TPU v7x, 1024 devices: a whole 4x8x16 slice. The times are simulated.
1024 devices in a mesh: fsdp: 16 (over z), tensor: 64 (over y, x, core).
Axes of the slice: x: 4, y: 8, z: 16, core: 2. Of those that a mesh axis runs over, the one named last changes fastest.
Arguments:
- momentum: float32 [16, 1152, 7168], P(None, 'fsdp', 'tensor'), may hold values from -600 to 600
- gradient: float32 [16, 1152, 7168], P(None, 'fsdp', 'tensor'), may hold values from -600 to 600
- live_ranks: int32 [16], replicated, may hold values from 0 to 1, as said below
- owner_group: int32 [16], replicated, may hold values from 0 to 15, each once
- row_counts: int32 [16, 16], replicated, may hold values from 1 to 72, as said below
- row_offsets: int32 [16, 16], replicated, may hold values from 0 to 575, as said below
Outputs:
- new_momentum: float32 [16, 1152, 7168], P(None, 'fsdp', 'tensor')
- update_shards: float32 [16, 1152, 7168], P(None, 'fsdp', 'tensor')
- owned_update: float32 [16, 576, 7168], P('fsdp', None, 'tensor')
Inputs may be any that keep to these rules, and one draw needn't show every extreme that they name: `live_ranks`: exactly one rank is dead. For every matrix the live ranks' segments [row_offsets, row_offsets + row_counts) are disjoint and cover all 576 rows, and one live rank holds exactly 72 rows. The dead rank's entries are stale and describe no rows. `row_offsets`: see row_counts.
All inputs are finite; a program needn't handle non-finite values.
Results may differ from a plain program's by a relative error of at most 0.0003.
Values sent between devices are 32-bit elements; how exact they have to be, the bound alone decides.
A program may use at most 32 MiB of HBM per device.

v0:
```python
import math

import jax
import jax.numpy as jnp
from jax import lax
from jax.sharding import PartitionSpec as P

WIDTH = 7168
INNER = 576
ITERS = 2


MOMENTUM_RATE = 0.95
QUINTIC_FIRST = 3.4445
QUINTIC_SECOND = -4.775
QUINTIC_THIRD = 2.0315
EPSILON = 1e-07
HIGHEST = lax.Precision.HIGHEST


def matmul(left_side, right_side):
    return jnp.dot(left_side, right_side, precision=HIGHEST, preferred_element_type=jnp.float32)


def gram_matrix(iterate):
    shares = lax.psum_scatter(
        lax.dot_general(
            iterate,
            iterate,
            (((1,), (1,)), ((), ())),
            precision=HIGHEST,
            preferred_element_type=jnp.float32,
        ),
        "tensor",
        scatter_dimension=0,
        tiled=True,
    )
    return lax.all_gather(shares, "tensor", axis=0, tiled=True)


def on_device(momentum, gradient, live_ranks, owner_group, row_counts, row_offsets):
    rank_count = lax.axis_size("fsdp")
    my_rank = lax.axis_index("fsdp")
    slot_count = momentum.shape[1]
    columns = momentum.shape[2]
    matrices = owner_group.shape[0]
    rank_ids = jnp.arange(rank_count, dtype=jnp.int32)
    matrix_ids = jnp.arange(matrices, dtype=jnp.int32)
    owned_by = jnp.sum(
        matrix_ids[None, :] * (owner_group[None, :] == rank_ids[:, None]).astype(jnp.int32), axis=1
    )
    position = jnp.arange(slot_count, dtype=jnp.int32)
    owned_matrix = lax.dynamic_index_in_dim(owned_by, my_rank, 0, keepdims=False)
    source_counts = (
        lax.dynamic_index_in_dim(row_counts, owned_matrix, 0, keepdims=False) * live_ranks
    )
    source_offsets = lax.dynamic_index_in_dim(row_offsets, owned_matrix, 0, keepdims=False)
    keep_in = position[None, :] < source_counts[:, None]
    target = jnp.where(keep_in, source_offsets[:, None] + position[None, :], INNER).reshape(-1)
    old_in, grad_in = (
        lax.all_to_all(
            jnp.take(momentum, owned_by, axis=0), "fsdp", split_axis=0, concat_axis=0, tiled=True
        ),
        lax.all_to_all(
            jnp.take(gradient, owned_by, axis=0), "fsdp", split_axis=0, concat_axis=0, tiled=True
        ),
    )
    fresh_in = MOMENTUM_RATE * old_in + grad_in
    blended_in = grad_in + MOMENTUM_RATE * fresh_in
    assembled = (
        jnp.zeros((INNER, columns), jnp.float32)
        .at[target]
        .add(blended_in.reshape(-1, columns), mode="drop")
    )
    square_total = lax.psum(jnp.sum(assembled * assembled), "tensor")
    iterate = assembled / (jnp.sqrt(square_total) + EPSILON)
    gram_now = gram_matrix(iterate)
    for repeat in range(ITERS):
        if repeat > 0:
            gram_now = gram_matrix(iterate)
        combined = QUINTIC_SECOND * gram_now + QUINTIC_THIRD * matmul(gram_now, gram_now)
        iterate = QUINTIC_FIRST * iterate + matmul(combined, iterate)
    result = iterate * (0.2 * math.sqrt(max(INNER, WIDTH)))
    picked = jnp.take(result, jnp.minimum(target, INNER - 1), axis=0).reshape(
        rank_count, slot_count, columns
    )
    sent_back = jnp.where(keep_in[:, :, None], picked, 0.0)
    fresh_back = jnp.where(keep_in[:, :, None], fresh_in, 0.0)
    update_home, momentum_home = (
        lax.all_to_all(sent_back, "fsdp", split_axis=0, concat_axis=0, tiled=True),
        lax.all_to_all(fresh_back, "fsdp", split_axis=0, concat_axis=0, tiled=True),
    )
    new_momentum = jnp.take(momentum_home, owner_group, axis=0)
    update_shards = jnp.take(update_home, owner_group, axis=0)
    return (new_momentum, update_shards, result[None])


def solution(mesh):
    placed = (P(None, "fsdp", "tensor"), P(None, "fsdp", "tensor"), P(), P(), P(), P())
    return jax.shard_map(
        on_device,
        mesh=mesh,
        in_specs=placed,
        out_specs=(P(None, "fsdp", "tensor"), P(None, "fsdp", "tensor"), P("fsdp", None, "tensor")),
        check_vma=False,
    )
```

profile of v0, /device:TPU:1, one launch (start us, length us, event | category | flops | bytes accessed | tf_op | source)
XLA Modules:
  0.0 937.9 jit_solution(11084801475687087942)
XLA Ops:
  10.4 52.1 %all_to_all.20 = f32[16,72,112]{2,1,0:T(8,128)S(1)} all-to-all(f32[16,72,112]{2,1,0:T(8,128)S(1)} %get-tuple-element.12), channel_id=1, replica_groups=mesh['fsdp'=16,'tensor'=64] {'fsdp'}, dimensions={0} | all-to-all | bytes 1032192 | tf_op jit(solution)/shard_map/all_to_all | solution.py:61
  62.5 5.3 all-to-all-start.1
  72.1 21.3 %all-to-all-done.1 = f32[16,72,112]{2,1,0:T(8,128)S(1)} async-done(((f32[16,72,112]{2,1,0:T(8,128)}), f32[16,72,112]{2,1,0:T(8,128)S(1)}, u32[]{:S(2)}, u32[]{:S(2)}) %all-to-all-start.1) | async-done | bytes 516128 | tf_op jit(solution)/shard_map/all_to_all | solution.py:64
  94.5 8.9 scatter_custom_fusion
  104.2 130.9 %psum.7 = f32[]{:T(128)} all-reduce(f32[]{:T(128)} %multiply_reduce_fusion), channel_id=1, replica_groups=mesh['fsdp'=16,'tensor'=64] {'tensor'}, use_global_device_ids=true, to_apply=%region_3.5 | all-reduce | flops 1 | bytes 8 | tf_op jit(solution)/shard_map/psum | solution.py:75
  235.8 2.5 fusion.24
  238.4 1.3 dynamic-slice
  240.3 213.4 %all-reduce.5.cloned.1.call-done = f32[576,576]{1,0:T(8,128)} async-done(((f32[576,576]{1,0:T(8,128)}), f32[576,576]{1,0:T(8,128)}) %all-reduce.5.cloned.1.call-update) | async-done | bytes 1327120
  453.7 1.5 dynamic-slice_bitcast_fusion.1
  455.4 97.0 %all-gather.5.cloned.1.call-done = f32[64,9,576]{2,1,0:T(8,128)} async-done(((f32[1,9,576]{2,1,0:T(8,128)}), f32[64,9,576]{2,1,0:T(8,128)}) %all-gather.5.cloned.1.call-update) | async-done | bytes 1327120 | tf_op jit(solution)/shard_map/all_gather | solution.py:38
  552.4 1.8 reshape.193
  554.2 4.2 fusion.31
  558.4 1.8 fusion.8
  560.2 2.5 fusion.32
  562.8 218.0 %all-reduce.7.cloned.1.call-done = f32[576,576]{1,0:T(8,128)} async-done(((f32[576,576]{1,0:T(8,128)}), f32[576,576]{1,0:T(8,128)}) %all-reduce.7.cloned.1.call-update) | async-done | bytes 1327120
  780.8 1.5 dynamic-slice_bitcast_fusion
  782.2 12.6 %all-to-all-start.2 = ((f32[16,72,112]{2,1,0:T(8,128)}), f32[16,72,112]{2,1,0:T(8,128)S(1)}, u32[]{:S(2)}, u32[]{:S(2)}) async-start(f32[16,72,112]{2,1,0:T(8,128)} %get-tuple-element.7), calls=%async_computation.2 | async-start | bytes 1179648 | tf_op jit(solution)/shard_map/all_to_all | solution.py:91
  794.8 84.5 %all-gather.7.cloned.1.call-done = f32[64,9,576]{2,1,0:T(8,128)} async-done(((f32[1,9,576]{2,1,0:T(8,128)}), f32[64,9,576]{2,1,0:T(8,128)}) %all-gather.7.cloned.1.call-update) | async-done | bytes 1327120 | tf_op jit(solution)/shard_map/all_gather | solution.py:38
  879.3 1.8 reshape.195
  881.2 4.2 fusion.33
  885.4 1.8 fusion.14
  887.3 2.4 gather_fusion
  891.0 12.7 %all-to-all-start.3 = ((f32[16,72,112]{2,1,0:T(8,128)}), f32[16,72,112]{2,1,0:T(8,128)S(1)}, u32[]{:S(2)}, u32[]{:S(2)}) async-start(f32[16,72,112]{2,1,0:T(8,128)} %select_select_fusion), calls=%async_computation.3 | async-start | bytes 1179648 | tf_op jit(solution)/shard_map/all_to_all | solution.py:90
  904.3 25.3 %all-to-all-done.3 = f32[16,72,112]{2,1,0:T(8,128)S(1)} async-done(((f32[16,72,112]{2,1,0:T(8,128)}), f32[16,72,112]{2,1,0:T(8,128)S(1)}, u32[]{:S(2)}, u32[]{:S(2)}) %all-to-all-start.3) | async-done | bytes 516128 | tf_op jit(solution)/shard_map/all_to_all | solution.py:90
  (45 shorter events, 11.4 us)
Async XLA Ops:
  7.2 1.1 copy-start
  7.2 1.7 copy-start.2
  10.4 60.7 %copy-start.3 = (s32[16]{0:T(128)S(1)}, s32[16]{0:T(128)}, u32[]{:S(2)}) copy-start(s32[16]{0:T(128)} %param.10) | copy-start | bytes 196
  62.5 30.9 %all-to-all-start.1 = ((f32[16,72,112]{2,1,0:T(8,128)}), f32[16,72,112]{2,1,0:T(8,128)S(1)}, u32[]{:S(2)}, u32[]{:S(2)}) async-start(f32[16,72,112]{2,1,0:T(8,128)} %get-tuple-element.13), calls=%async_computation.1 | async-start | bytes 1179648 | tf_op jit(solution)/shard_map/all_to_all | solution.py:64
  67.8 385.9 %all-reduce.5.cloned.1.call-start = ((), (), s32[]{:S(2)}) async-start(), calls=%async_computation.6 | async-start | bytes 2949120
  238.3 314.1 %all-gather.5.cloned.1.call-start = ((), (), s32[]{:S(2)}) async-start(), calls=%async_computation.4 | async-start | bytes 2662400 | tf_op jit(solution)/shard_map/all_gather | solution.py:38
  455.1 325.6 %all-reduce.7.cloned.1.call-start = ((), (), s32[]{:S(2)}) async-start(), calls=%async_computation.7 | async-start | bytes 2949120
  562.7 316.6 %all-gather.7.cloned.1.call-start = ((), (), s32[]{:S(2)}) async-start(), calls=%async_computation.5 | async-start | bytes 2662400 | tf_op jit(solution)/shard_map/all_gather | solution.py:38
  782.2 108.7 %all-to-all-start.2 = ((f32[16,72,112]{2,1,0:T(8,128)}), f32[16,72,112]{2,1,0:T(8,128)S(1)}, u32[]{:S(2)}, u32[]{:S(2)}) async-start(f32[16,72,112]{2,1,0:T(8,128)} %get-tuple-element.7), calls=%async_computation.2 | async-start | bytes 1179648 | tf_op jit(solution)/shard_map/all_to_all | solution.py:91
  887.1 2.6 copy-start.1
  889.8 13.9 %copy-start.4 = (s32[16]{0:T(128)S(1)}, s32[16]{0:T(128)}, u32[]{:S(2)}) copy-start(s32[16]{0:T(128)} %param.11) | copy-start | bytes 196
  891.0 38.6 %all-to-all-start.3 = ((f32[16,72,112]{2,1,0:T(8,128)}), f32[16,72,112]{2,1,0:T(8,128)S(1)}, u32[]{:S(2)}, u32[]{:S(2)}) async-start(f32[16,72,112]{2,1,0:T(8,128)} %select_select_fusion), calls=%async_computation.3 | async-start | bytes 1179648 | tf_op jit(solution)/shard_map/all_to_all | solution.py:90
Sparse Core Ops, SparseCore 0:
  238.4 215.1 all-reduce.4
  458.7 93.6 all-gather.4
  562.8 217.8 all-reduce.6
  785.7 93.6 all-gather.6
where the time goes:
time: 943 us; the launch traced here: 938 us
  waiting for transfers between devices  660 us (70%)
  blocking collectives  183 us (19%)
  starting transfers between devices  30.9 us (3%)
  between operations  17.3 us (2%)
  matrix products  16.9 us (2%)
  other arithmetic  15.7 us (2%)
  local copies, waits for them, and re-layouts  14.4 us (2%)
    unnamed x6, waiting for transfers between devices  431 us
    all_gather x2, waiting for transfers between devices, gram_matrix(): return lax.all_gather(shares, 'tensor', axis=0, tiled=True)  182 us
    psum x1, blocking collectives, on_device(): square_total = lax.psum(jnp.sum(assembled * assembled), 'tensor')  131 us
    all_to_all x1, blocking collectives, on_device(): lax.all_to_all(jnp.take(momentum, owned_by, axis=0), 'fsdp', split_axis=0...  52.1 us
    all_to_all x1, waiting for transfers between devices, on_device(): lax.all_to_all(sent_back, 'fsdp', split_axis=0, concat_axis=0, tiled=True)  25.3 us
    all_to_all x1, waiting for transfers between devices, on_device(): lax.all_to_all(jnp.take(gradient, owned_by, axis=0), 'fsdp', split_axis=0...  21.3 us
  transfers between devices with their start and end apart: 7, of which 6 were waited for; matrix products, arithmetic and copies ran while one was open for 2% of the time, Pallas kernels for 0%

commit v1 on v0

v1 whole, which is shorter than its diff:
```python
import math

import jax
import jax.numpy as jnp
from jax import lax
from jax.sharding import PartitionSpec as P

WIDTH = 7168
INNER = 576

MOMENTUM_RATE = 0.95
QUINTIC_FIRST = 3.4445
QUINTIC_SECOND = -4.775
QUINTIC_THIRD = 2.0315
EPSILON = 1e-07
HIGH = lax.Precision.HIGH


def matmul(left_side, right_side, precision=HIGH):
    return jnp.dot(left_side, right_side, precision=precision, preferred_element_type=jnp.float32)


def on_device(momentum, gradient, live_ranks, owner_group, row_counts, row_offsets):
    rank_count = lax.axis_size("fsdp")
    my_rank = lax.axis_index("fsdp")
    slot_count = momentum.shape[1]
    columns = momentum.shape[2]
    matrices = owner_group.shape[0]
    rank_ids = jnp.arange(rank_count, dtype=jnp.int32)
    matrix_ids = jnp.arange(matrices, dtype=jnp.int32)
    owned_by = jnp.sum(
        matrix_ids[None, :] * (owner_group[None, :] == rank_ids[:, None]).astype(jnp.int32), axis=1
    )
    position = jnp.arange(slot_count, dtype=jnp.int32)
    counts = row_counts * live_ranks[None, :]
    my_counts = lax.dynamic_index_in_dim(counts, my_rank, 1, keepdims=False)
    valid = (position[None, :] < my_counts[:, None])[:, :, None]
    new_momentum = jnp.where(valid, MOMENTUM_RATE * momentum + gradient, 0.0)
    blended = jnp.where(valid, gradient + MOMENTUM_RATE * new_momentum, 0.0)
    blended_in = lax.all_to_all(
        jnp.take(blended, owned_by, axis=0), "fsdp", split_axis=0, concat_axis=0, tiled=True
    )
    owned_matrix = lax.dynamic_index_in_dim(owned_by, my_rank, 0, keepdims=False)
    source_counts = lax.dynamic_index_in_dim(counts, owned_matrix, 0, keepdims=False)
    source_offsets = lax.dynamic_index_in_dim(row_offsets, owned_matrix, 0, keepdims=False)
    keep_in = position[None, :] < source_counts[:, None]
    target = jnp.where(keep_in, source_offsets[:, None] + position[None, :], -1).reshape(-1)
    select = (target[None, :] == jnp.arange(INNER, dtype=jnp.int32)[:, None]).astype(jnp.float32)
    assembled = matmul(select, blended_in.reshape(-1, columns), lax.Precision.HIGHEST)
    gram = lax.dot_general(
        assembled,
        assembled,
        (((1,), (1,)), ((), ())),
        precision=HIGH,
        preferred_element_type=jnp.float32,
    )
    shares = lax.psum_scatter(gram, "tensor", scatter_dimension=0, tiled=True)
    gram = lax.all_gather(shares, "tensor", axis=0, tiled=True)
    inverse = 1.0 / (jnp.sqrt(jnp.trace(gram)) + EPSILON)
    gram = (gram * inverse) * inverse
    eye = jnp.eye(INNER, dtype=jnp.float32)

    def step(gram_now):
        return (
            QUINTIC_FIRST * eye
            + QUINTIC_SECOND * gram_now
            + QUINTIC_THIRD * matmul(gram_now, gram_now)
        )

    first = step(gram)
    second = step(matmul(matmul(first, gram), first))
    result = matmul(second, matmul(first, assembled * inverse)) * (
        0.2 * math.sqrt(max(INNER, WIDTH))
    )
    sent_back = lax.dot_general(
        select,
        result,
        (((0,), (0,)), ((), ())),
        precision=lax.Precision.HIGHEST,
        preferred_element_type=jnp.float32,
    ).reshape(rank_count, slot_count, columns)
    update_home = lax.all_to_all(sent_back, "fsdp", split_axis=0, concat_axis=0, tiled=True)
    update_shards = jnp.take(update_home, owner_group, axis=0)
    return (new_momentum, update_shards, result[None])


def solution(mesh):
    placed = (P(None, "fsdp", "tensor"), P(None, "fsdp", "tensor"), P(), P(), P(), P())
    return jax.shard_map(
        on_device,
        mesh=mesh,
        in_specs=placed,
        out_specs=(P(None, "fsdp", "tensor"), P(None, "fsdp", "tensor"), P("fsdp", None, "tensor")),
        check_vma=False,
    )
```

time: 943 us -> 451 us (0.48)
  waiting for transfers between devices: 660 us -> 365 us
  blocking collectives: 183 us -> 0 us
    unnamed x6 -> x3, waiting for transfers between devices: 431 us -> 220 us
    psum x1 -> x0, blocking collectives: 131 us -> none  [on_device(): square_total = lax.psum(jnp.sum(assembled * assembled), 'tensor')]
    all_gather x2 -> x1, waiting for transfers between devices: 182 us -> 97.3 us  [on_device(): gram = lax.all_gather(shares, 'tensor', axis=0, tiled=True)]
    all_to_all x1 -> x0, blocking collectives: 52.1 us -> none  [on_device(): lax.all_to_all(jnp.take(momentum, owned_by, axis=0), 'fsdp', split_axis=0...]
    all_to_all x2 -> x1, starting transfers between devices: 17.9 us -> 19.4 us  [on_device(): lax.all_to_all(jnp.take(blended, owned_by, axis=0), 'fsdp', split_axis=0,...]
    all_to_all x2 -> x1, waiting for transfers between devices: 21.3 us -> 21.9 us  [on_device(): lax.all_to_all(jnp.take(blended, owned_by, axis=0), 'fsdp', split_axis=0,...]
  transfers between devices with their start and end apart: 7 -> 4, of which waited for: 6 -> 4; matrix products, arithmetic and copies ran while one was open for 2% -> 1% of each run, Pallas kernels for 0% -> 0%
where the time goes in v1:
time: 451 us; the launch traced here: 446 us
  waiting for transfers between devices  365 us (81%)
  starting transfers between devices  32.2 us (7%)
  between operations  17.5 us (4%)
  matrix products  16.7 us (4%)
  local copies, waits for them, and re-layouts  7.44 us (2%)
  other arithmetic  6.48 us (1%)
    unnamed x3, waiting for transfers between devices  220 us
    all_gather x1, waiting for transfers between devices, on_device(): gram = lax.all_gather(shares, 'tensor', axis=0, tiled=True)  97.3 us
    all_to_all x1, waiting for transfers between devices, on_device(): lax.all_to_all(sent_back, 'fsdp', split_axis=0, concat_axis=0, tiled=True)  25.9 us
    all_to_all x1, waiting for transfers between devices, on_device(): lax.all_to_all(jnp.take(blended, owned_by, axis=0), 'fsdp', split_axis=0,...  21.9 us
    all_to_all x1, starting transfers between devices, on_device(): lax.all_to_all(jnp.take(blended, owned_by, axis=0), 'fsdp', split_axis=0,...  19.4 us
    all_to_all x1, starting transfers between devices, on_device(): lax.all_to_all(sent_back, 'fsdp', split_axis=0, concat_axis=0, tiled=True)  12.7 us
    dot_general x7, matrix products, matmul(): jnp.dot(left_side, right_side, precision=precision, preferred_element_typ...  12.3 us
  transfers between devices with their start and end apart: 4, of which 4 were waited for; matrix products, arithmetic and copies ran while one was open for 1% of the time, Pallas kernels for 0%

profile of v1, /device:TPU:1, one launch (start us, length us, event | category | flops | bytes accessed | tf_op | source)
XLA Modules:
  0.0 445.7 jit_solution(14028718954028046625)
XLA Ops:
  7.2 0.8 select_reduce_fusion.1
  8.0 0.7 broadcast_multiply_fusion
  8.9 2.3 add_select_fusion
  11.8 0.9 broadcast_select_fusion.1
  12.7 19.4 %all-to-all-start = ((f32[16,72,112]{2,1,0:T(8,128)}), f32[16,72,112]{2,1,0:T(8,128)S(1)}, u32[]{:S(2)}, u32[]{:S(2)}) async-start(f32[16,72,112]{2,1,0:T(8,128)} %broadcast_select_fusion.1), calls=%async_computation | async-start | bytes 1179648 | tf_op jit(solution)/shard_map/all_to_all | solution.py:40
  34.7 0.7 fusion.25
  35.6 21.9 %all-to-all-done = f32[16,72,112]{2,1,0:T(8,128)S(1)} async-done(((f32[16,72,112]{2,1,0:T(8,128)}), f32[16,72,112]{2,1,0:T(8,128)S(1)}, u32[]{:S(2)}, u32[]{:S(2)}) %all-to-all-start) | async-done | bytes 516128 | tf_op jit(solution)/shard_map/all_to_all | solution.py:40
  57.5 1.5 fusion.1
  59.0 1.9 fusion.31
  61.0 1.3 dynamic-slice
  62.9 220.3 %all-reduce.3.cloned.1.call-done = f32[576,576]{1,0:T(8,128)} async-done(((f32[576,576]{1,0:T(8,128)}), f32[576,576]{1,0:T(8,128)}) %all-reduce.3.cloned.1.call-update) | async-done | bytes 1327120
  283.2 1.5 dynamic-slice_bitcast_fusion
  284.7 97.3 %all-gather.3.cloned.1.call-done = f32[64,9,576]{2,1,0:T(8,128)} async-done(((f32[1,9,576]{2,1,0:T(8,128)}), f32[64,9,576]{2,1,0:T(8,128)}) %all-gather.3.cloned.1.call-update) | async-done | bytes 1327120 | tf_op jit(solution)/shard_map/all_gather | solution.py:58
  382.0 2.0 reshape.97
  385.4 2.2 fusion.2
  387.6 0.8 fusion.22
  388.5 2.2 fusion.12
  390.7 2.2 fusion.32
  392.9 2.2 fusion.33
  395.2 1.0 fusion.13
  396.2 2.6 fusion.8
  398.8 12.7 %all-to-all-start.1 = ((f32[16,72,112]{2,1,0:T(8,128)}), f32[16,72,112]{2,1,0:T(8,128)S(1)}, u32[]{:S(2)}, u32[]{:S(2)}) async-start(f32[16,72,112]{2,1,0:T(8,128)} %bitcast.5), calls=%async_computation.1 | async-start | bytes 1179648 | tf_op jit(solution)/shard_map/all_to_all | solution.py:82
  411.5 25.9 %all-to-all-done.1 = f32[16,72,112]{2,1,0:T(8,128)S(1)} async-done(((f32[16,72,112]{2,1,0:T(8,128)}), f32[16,72,112]{2,1,0:T(8,128)S(1)}, u32[]{:S(2)}, u32[]{:S(2)}) %all-to-all-start.1) | async-done | bytes 516128 | tf_op jit(solution)/shard_map/all_to_all | solution.py:82
  438.0 0.9 broadcast_select_fusion
  (22 shorter events, 3.0 us)
Async XLA Ops:
  12.7 44.8 %all-to-all-start = ((f32[16,72,112]{2,1,0:T(8,128)}), f32[16,72,112]{2,1,0:T(8,128)S(1)}, u32[]{:S(2)}, u32[]{:S(2)}) async-start(f32[16,72,112]{2,1,0:T(8,128)} %broadcast_select_fusion.1), calls=%async_computation | async-start | bytes 1179648 | tf_op jit(solution)/shard_map/all_to_all | solution.py:40
  32.2 251.1 %all-reduce.3.cloned.1.call-start = ((), (), s32[]{:S(2)}) async-start(), calls=%async_computation.3 | async-start | bytes 2949120
  61.0 321.0 %all-gather.3.cloned.1.call-start = ((), (), s32[]{:S(2)}) async-start(), calls=%async_computation.2 | async-start | bytes 2662400 | tf_op jit(solution)/shard_map/all_gather | solution.py:58
  396.2 41.8 %copy-start = (f32[576,112]{0,1:T(8,128)}, f32[576,112]{0,1:T(8,128)S(1)}, u32[]{:S(2)}) copy-start(f32[576,112]{0,1:T(8,128)S(1)} %fusion.13) | copy-start | bytes 774148
  396.2 15.3 %copy-start.1 = (s32[16]{0:T(128)S(1)}, s32[16]{0:T(128)}, u32[]{:S(2)}) copy-start(s32[16]{0:T(128)} %param.11) | copy-start | bytes 196
  398.8 38.6 %all-to-all-start.1 = ((f32[16,72,112]{2,1,0:T(8,128)}), f32[16,72,112]{2,1,0:T(8,128)S(1)}, u32[]{:S(2)}, u32[]{:S(2)}) async-start(f32[16,72,112]{2,1,0:T(8,128)} %bitcast.5), calls=%async_computation.1 | async-start | bytes 1179648 | tf_op jit(solution)/shard_map/all_to_all | solution.py:82
Sparse Core Ops, SparseCore 0:
  61.1 222.0 all-reduce.2
  288.3 93.6 all-gather.2

commit v2 on v1

v2 whole, which is shorter than its diff:
```python
import functools
import math

import jax
import jax.numpy as jnp
from jax import lax
from jax.experimental import pallas as pl
from jax.experimental.pallas import tpu as pltpu
from jax.sharding import PartitionSpec as P

WIDTH = 7168
INNER = 576
PADDED = 640
BLOCK = 64
LANES = 128

MOMENTUM_RATE = 0.95
QUINTIC_FIRST = 3.4445
QUINTIC_SECOND = -4.775
QUINTIC_THIRD = 2.0315
EPSILON = 1e-07
SCALE = 0.2 * math.sqrt(max(INNER, WIDTH))

MESH = pl.DeviceIdType.MESH
F32 = jnp.float32
BF16 = jnp.bfloat16

GRID = (8, 4, 2)


def dot(left, right):
    return jnp.dot(left, right, preferred_element_type=F32)


def iota(shape, axis):
    return lax.broadcasted_iota(jnp.int32, shape, axis)


def split(value):
    high = value.astype(BF16)
    low = (value - high.astype(F32)).astype(BF16)
    return high, low


def pack_slots(block):
    rows, columns = block.shape
    spare = LANES - columns
    wide = jnp.concatenate([block, jnp.zeros((rows, spare), F32)], axis=1)
    last = wide[rows - 8 :]
    pieces = []
    for tile in range((rows - 8) // 8):
        if tile * spare < columns:
            pieces.append(pltpu.roll(last, (columns - spare * tile) % LANES, 1))
        else:
            pieces.append(jnp.zeros((8, LANES), F32))
    tail = jnp.concatenate(pieces, axis=0)
    return jnp.where(iota(tail.shape, 1) < columns, wide[: rows - 8], tail)


def unpack_slots(packed, columns):
    spare = LANES - columns
    lane = iota((8, LANES), 1)
    last = jnp.zeros((8, LANES), F32)
    for tile in range(-(-columns // spare)):
        piece = pltpu.roll(packed[8 * tile : 8 * tile + 8], (spare * tile - columns) % LANES, 1)
        last = jnp.where((lane >= spare * tile) & (lane < spare * (tile + 1)), piece, last)
    main = jnp.where(iota(packed.shape, 1) < columns, packed, 0.0)
    return jnp.concatenate([main, last], axis=0)


def pack_gram(gram, store):
    lane = iota((BLOCK, LANES), 1)

    def tile(row, column):
        return gram[BLOCK * row : BLOCK * row + BLOCK, LANES * column : LANES * column + LANES]

    entry = 0
    for p in range(4):
        for column in range(p, 4):
            store(entry, tile(2 * p, column))
            entry += 1
        for column in range(p + 1, 4):
            store(entry, tile(2 * p + 1, column))
            entry += 1
        store(entry, jnp.where(lane < BLOCK, tile(2 * p, 4), tile(2 * p + 1, p)))
        entry += 1
    for row in (1, 5):
        store(entry, jnp.where(lane < BLOCK, tile(row, 4), pltpu.roll(tile(row + 2, 4), BLOCK, 1)))
        entry += 1
    store(entry, tile(8, 4))


ENTRIES = 23


def gram_entries():
    full, merged, entry = {}, {}, 0
    for p in range(4):
        for column in range(p, 4):
            full[2 * p, column] = entry
            entry += 1
        for column in range(p + 1, 4):
            full[2 * p + 1, column] = entry
            entry += 1
        merged[p] = entry
        entry += 1
    return full, merged, {1: entry, 5: entry + 1}, entry + 2


def gram_trace(load):
    full, merged, _, last = gram_entries()
    row, lane = iota((BLOCK, LANES), 0), iota((BLOCK, LANES), 1)
    diagonal = row == lane
    total = jnp.where(diagonal, load(last), 0.0)
    for p in range(4):
        total += jnp.where(diagonal, load(full[2 * p, p]), 0.0)
        total += jnp.where(row + BLOCK == lane, load(merged[p]), 0.0)
    return jnp.sum(total, axis=(0, 1), keepdims=True)


def unpack_gram(load, store):
    full, merged, edge, last = gram_entries()
    half = iota((BLOCK, LANES), 1) < BLOCK
    row, lane = iota((LANES, LANES), 0), iota((LANES, LANES), 1)
    for p in range(4):
        block = jnp.concatenate(
            [load(full[2 * p, p]), jnp.where(half, 0.0, load(merged[p]))], axis=0
        )
        store(p, p, jnp.where((row >= BLOCK) & (lane < BLOCK), block.T, block))
        for q in range(p + 1, 4):
            block = jnp.concatenate([load(full[2 * p, q]), load(full[2 * p + 1, q])], axis=0)
            store(p, q, block)
            store(q, p, block.T)
        odd = 2 * p + 1
        if odd in edge:
            right = load(edge[odd])
        else:
            right = pltpu.roll(load(edge[odd - 2]), BLOCK, 1)
        block = jnp.concatenate(
            [jnp.where(half, load(merged[p]), 0.0), jnp.where(half, right, 0.0)], axis=0
        )
        store(p, 4, block)
        store(4, p, block.T[:BLOCK])
    store(4, 4, jnp.where(half, load(last), 0.0))


def near_first(count):
    order = [0]
    for distance in range(1, count // 2 + 1):
        order.append(distance)
        if distance != count - distance:
            order.append(count - distance)
    return order


def step_kernel(
    ranks,
    grid,
    momentum,
    gradient,
    live,
    owners,
    counts,
    offsets,
    home,
    result,
    sent_in,
    came_in,
    sent_out,
    gathered,
    gram,
    part,
    other,
    row_sum,
    row_in,
    cell_sum,
    cell_in,
    whole,
    halves,
    column,
    kept,
    summed,
    in_send,
    in_recv,
    out_send,
    out_recv,
    core_send,
    core_recv,
    x_send,
    x_recv,
    y_send,
    y_recv,
):
    y_count, x_count, core_count = grid
    matrices, slots, columns = momentum.shape
    me = lax.axis_index("fsdp")
    here = lax.axis_index("tensor")
    core = lax.rem(here, core_count)
    x_here = lax.rem(here // core_count, x_count)
    y_here = here // (core_count * x_count)

    def rank_at(distance):
        return {"fsdp": lax.rem(me + distance, ranks), "tensor": here}

    def cell(y, x, c):
        return {"fsdp": me, "tensor": (y * x_count + x) * core_count + c}

    sibling = cell(y_here, x_here, 1 - core)
    x_peers = [cell(y_here, lax.rem(x_here + d, x_count), core) for d in range(1, x_count)]
    y_peers = [cell(lax.rem(y_here + d, y_count), x_here, core) for d in range(1, y_count)]

    barrier = pltpu.get_barrier_semaphore()
    peers = [rank_at(d) for d in range(1, ranks)] + [sibling] + x_peers + y_peers
    for peer in peers:
        pl.semaphore_signal(barrier, inc=1, device_id=peer, device_id_type=MESH)

    def owned_by(rank):
        found = jnp.int32(0)
        for k in range(matrices):
            found = jnp.where(owners[k] == rank, k, found)
        return found

    mine = owned_by(me)
    for d in range(ranks):
        k = mine if d == 0 else owned_by(lax.rem(me + d, ranks))
        grad = gradient[k]
        blended = grad + MOMENTUM_RATE * (MOMENTUM_RATE * momentum[k] + grad)
        if d == 0:
            came_in[0] = pack_slots(blended)
        else:
            sent_in[d] = pack_slots(blended)

    pl.semaphore_wait(barrier, len(peers))

    order = near_first(ranks)
    copies_in = {}
    for d in order[:0:-1]:
        copies_in[d] = pltpu.make_async_remote_copy(
            src_ref=sent_in.at[d],
            dst_ref=came_in.at[d],
            send_sem=in_send.at[d],
            recv_sem=in_recv.at[d],
            device_id=rank_at(d),
            device_id_type=MESH,
        )
        copies_in[d].start()

    def held(rank):
        return offsets[mine, rank], counts[mine, rank] * live[rank]

    for pair in range(ranks // 2):
        blocks, tables = [], []
        for d in order[2 * pair : 2 * pair + 2]:
            if d > 0:
                copies_in[d].wait_recv()
            blocks.append(unpack_slots(came_in[d], columns))
            tables.append(held(lax.rem(me + ranks - d, ranks)))
        data = jnp.concatenate(split(jnp.concatenate(blocks, axis=0)), axis=1)
        lane = iota((INNER, 2 * slots), 1)
        first = lane < slots
        slot = jnp.where(first, lane, lane - slots)
        offset = jnp.where(first, tables[0][0], tables[1][0])
        count = jnp.where(first, tables[0][1], tables[1][1])
        select = (iota((INNER, 2 * slots), 0) - slot == offset) & (slot < count)
        added = dot(jnp.where(select, 1.0, 0.0).astype(BF16), data)
        if pair == 0:
            gathered[...] = added
        else:
            gathered[...] += added

    both = gathered[...].astype(BF16)
    high, low = both[:, :LANES], both[:, LANES:]
    pad = jnp.zeros((PADDED - INNER, 4 * LANES), BF16)
    left = jnp.concatenate([both, both], axis=1)
    right = jnp.concatenate([jnp.concatenate([high, high, low, low], axis=1), pad], axis=0)
    across = (((1,), (1,)), ((), ()))
    cut = 2 * LANES
    gram[:cut, :] = lax.dot_general(left[:cut], right, across, preferred_element_type=F32)
    gram[cut:, cut:] = lax.dot_general(left[cut:], right[cut:], across, preferred_element_type=F32)

    def put(entry, tile):
        part[BLOCK * entry : BLOCK * entry + BLOCK, :] = tile

    pack_gram(gram, put)
    total_rows = part.shape[0]
    if total_rows > BLOCK * ENTRIES:
        part[BLOCK * ENTRIES :, :] = jnp.zeros((total_rows - BLOCK * ENTRIES, LANES), F32)

    piece = total_rows // (core_count * y_count * x_count)

    def place(ref, index, count=1):
        size = piece * count
        return ref.at[pl.ds(pl.multiple_of(index * piece, 8), size), :]

    pending = []

    def send(src, dst, peer, send_sem, recv_sem):
        copy = pltpu.make_async_remote_copy(
            src_ref=src,
            dst_ref=dst,
            send_sem=send_sem,
            recv_sem=recv_sem,
            device_id=peer,
            device_id_type=MESH,
        )
        copy.start()
        pending.append(copy)
        return copy

    cells = y_count * x_count
    y_order = near_first(y_count)
    x_order = near_first(x_count)[1:]

    def y_at(d):
        return lax.rem(y_here + d, y_count)

    def x_at(d):
        return lax.rem(x_here + d, x_count)

    copies = {}
    for d in y_order[::-1]:
        line = y_at(d) * x_count
        copies[d] = send(
            place(part, (1 - core) * cells + line, x_count),
            place(other, line, x_count),
            sibling,
            core_send.at[d],
            core_recv.at[d],
        )
    x_copies = {}
    for d in y_order[::-1]:
        line = y_at(d) * x_count
        copies[d].wait_recv()
        place(row_sum, line, x_count)[...] = (
            place(part, core * cells + line, x_count)[...] + place(other, line, x_count)[...]
        )
        for e in x_order[::-1]:
            slot = d * x_count + e
            x_copies[d, e] = send(
                place(row_sum, line + x_at(e)),
                row_in.at[slot],
                x_peers[e - 1],
                x_send.at[slot],
                x_recv.at[slot],
            )
    y_copies = {}
    for d in y_order[::-1]:
        total = place(row_sum, y_at(d) * x_count + x_here)[...]
        for e in x_order:
            x_copies[d, e].wait_recv()
            total = total + row_in[d * x_count + e]
        if d == 0:
            own_total = total
        else:
            cell_sum[d] = total
            y_copies[d] = send(
                cell_sum.at[d], cell_in.at[d], y_peers[d - 1], y_send.at[d], y_recv.at[d]
            )
    total = own_total
    for d in y_order[1:]:
        y_copies[d].wait_recv()
        total = total + cell_in[d]

    def home_of(d, e):
        return place(whole, core * cells + y_at(d) * x_count + x_at(e))

    home_of(0, 0)[...] = total
    for d in y_order[:0:-1]:
        y_copies[d] = send(
            home_of(0, 0),
            home_of(0, 0),
            y_peers[d - 1],
            y_send.at[y_count + d],
            y_recv.at[y_count + d],
        )
    core_copies = []
    for d in y_order:
        back = lax.rem(y_count - d, y_count)
        if d > 0:
            y_copies[d].wait_recv()
        for e in x_order[::-1]:
            slot = (y_count + d) * x_count + e
            x_copies[d, e] = send(
                home_of(back, 0),
                home_of(back, 0),
                x_peers[e - 1],
                x_send.at[slot],
                x_recv.at[slot],
            )
        slot = y_count + d * x_count
        core_copies.append(
            send(
                home_of(back, 0), home_of(back, 0), sibling, core_send.at[slot], core_recv.at[slot]
            )
        )
    for d in y_order:
        back = lax.rem(y_count - d, y_count)
        for e in x_order:
            x_copies[d, e].wait_recv()
            source = home_of(back, x_count - e)
            slot = y_count + d * x_count + e
            core_copies.append(
                send(source, source, sibling, core_send.at[slot], core_recv.at[slot])
            )
    for copy in core_copies:
        copy.wait_recv()

    def load(entry):
        return whole[BLOCK * entry : BLOCK * entry + BLOCK, :]

    inverse = 1.0 / (jnp.sqrt(gram_trace(load)) + EPSILON)

    def keep(p, q, block):
        high, low = split((block * inverse) * inverse)
        rows, lanes = slice(LANES * p, LANES * p + block.shape[0]), LANES * q
        halves[rows, lanes : lanes + LANES] = high
        halves[rows, PADDED + lanes : PADDED + lanes + LANES] = low

    unpack_gram(load, keep)

    for base in (0, PADDED):
        column[base + INNER : base + PADDED, :] = jnp.zeros((PADDED - INNER, 2 * LANES), BF16)

    def stack(value):
        both = jnp.concatenate(split(value), axis=1)
        column[:INNER, :] = both
        column[PADDED : PADDED + INNER, :] = both

    start = (gathered[:, :LANES] + gathered[:, LANES:]) * inverse
    kept[...] = start
    summed[...] = jnp.zeros_like(start)
    stack(start)

    @pl.loop(0, 12)
    def _(index):
        phase = lax.rem(index + 3, 5)
        opens = (phase == 3) | (phase == 1)
        closes = (phase == 4) | (phase == 2)
        keep_part = jnp.where(opens, QUINTIC_SECOND, jnp.where(closes, QUINTIC_FIRST, 0.0))
        product_part = jnp.where(opens, QUINTIC_THIRD, 1.0)
        sum_part = jnp.where(
            index == 1,
            QUINTIC_FIRST,
            jnp.where(index == 6, QUINTIC_SECOND, jnp.where(index == 11, QUINTIC_THIRD, 0.0)),
        )
        product = dot(halves[...], column[...])
        value = keep_part * kept[...] + product_part * (product[:, :LANES] + product[:, LANES:])
        stack(value)
        kept[...] = jnp.where(opens, kept[...], value)
        summed[...] += sum_part * value

    final = summed[...] * SCALE
    result[...] = final
    stack(final)
    sent = column[:PADDED, :]
    backward = order[::-1]
    copies_out = []
    for pair in range(ranks // 2):
        ds = backward[2 * pair : 2 * pair + 2]
        tables = [held(lax.rem(me + d, ranks)) for d in ds]
        row = iota((2 * slots, PADDED), 0)
        first = row < slots
        slot = jnp.where(first, row, row - slots)
        offset = jnp.where(first, tables[0][0], tables[1][0])
        count = jnp.where(first, tables[0][1], tables[1][1])
        select = (iota((2 * slots, PADDED), 1) - slot == offset) & (slot < count)
        picked = dot(jnp.where(select, 1.0, 0.0).astype(BF16), sent)
        picked = (picked[:, :LANES] + picked[:, LANES:])[:, :columns]
        for place, d in enumerate(ds):
            packed = pack_slots(picked[place * slots : place * slots + slots])
            if d == 0:
                home[0] = packed
                continue
            sent_out[d] = packed
            copy = pltpu.make_async_remote_copy(
                src_ref=sent_out.at[d],
                dst_ref=home.at[d],
                send_sem=out_send.at[d],
                recv_sem=out_recv.at[d],
                device_id=rank_at(d),
                device_id_type=MESH,
            )
            copy.start()
            copies_out.append(copy)
    for copy in copies_out:
        copy.wait_recv()
    for copy in list(copies_in.values()) + pending + copies_out:
        copy.wait_send()


def finish_kernel(ranks, columns, home, result, owners, update, owned):
    me = lax.axis_index("fsdp")
    for k in range(update.shape[0]):
        source = lax.rem(me + ranks - owners[k], ranks)
        update[k] = unpack_slots(home[source], columns)[:, :columns]
    owned[0] = result[:, :columns]


def on_device(ranks, grid, momentum, gradient, live_ranks, owner_group, row_counts, row_offsets):
    y_count, x_count, core_count = grid
    matrices, slots, columns = momentum.shape
    cells = y_count * x_count * core_count
    piece = -(-8 * ENTRIES // cells) * 8
    total_rows = piece * cells
    half_rows = total_rows // core_count

    vmem = pl.BlockSpec(memory_space=pltpu.VMEM)
    smem = pl.BlockSpec(memory_space=pltpu.SMEM)
    packed = (ranks, slots - 8, LANES)
    dma = pltpu.SemaphoreType.DMA
    home, result = pl.pallas_call(
        functools.partial(step_kernel, ranks, grid),
        out_shape=(jax.ShapeDtypeStruct(packed, F32), jax.ShapeDtypeStruct((INNER, LANES), F32)),
        in_specs=[vmem, vmem, smem, smem, smem, smem],
        out_specs=(vmem, vmem),
        scratch_shapes=[
            pltpu.VMEM(packed, F32),
            pltpu.VMEM(packed, F32),
            pltpu.VMEM(packed, F32),
            pltpu.VMEM((INNER, 2 * LANES), F32),
            pltpu.VMEM((INNER, PADDED), F32),
            pltpu.VMEM((total_rows, LANES), F32),
            pltpu.VMEM((half_rows, LANES), F32),
            pltpu.VMEM((half_rows, LANES), F32),
            pltpu.VMEM((y_count * x_count, piece, LANES), F32),
            pltpu.VMEM((y_count, piece, LANES), F32),
            pltpu.VMEM((y_count, piece, LANES), F32),
            pltpu.VMEM((total_rows, LANES), F32),
            pltpu.VMEM((INNER, 2 * PADDED), BF16),
            pltpu.VMEM((2 * PADDED, 2 * LANES), BF16),
            pltpu.VMEM((INNER, LANES), F32),
            pltpu.VMEM((INNER, LANES), F32),
            dma((ranks,)),
            dma((ranks,)),
            dma((ranks,)),
            dma((ranks,)),
            dma((y_count * (1 + x_count),)),
            dma((y_count * (1 + x_count),)),
            dma((2 * y_count * x_count,)),
            dma((2 * y_count * x_count,)),
            dma((2 * y_count,)),
            dma((2 * y_count,)),
        ],
        compiler_params=pltpu.CompilerParams(collective_id=0, has_side_effects=True),
        name="muon_exchange",
    )(momentum, gradient, live_ranks, owner_group, row_counts, row_offsets)

    update_shards, owned_update = pl.pallas_call(
        functools.partial(finish_kernel, ranks, columns),
        out_shape=(
            jax.ShapeDtypeStruct(momentum.shape, F32),
            jax.ShapeDtypeStruct((1, INNER, columns), F32),
        ),
        in_specs=[vmem, vmem, smem],
        out_specs=(vmem, vmem),
        name="muon_finish",
    )(home, result, owner_group)

    my_rank = lax.axis_index("fsdp")
    my_counts = lax.dynamic_index_in_dim(row_counts * live_ranks[None, :], my_rank, 1, keepdims=False)
    valid = jnp.arange(slots, dtype=jnp.int32)[None, :] < my_counts[:, None]
    new_momentum = jnp.where(valid[:, :, None], MOMENTUM_RATE * momentum + gradient, 0.0)
    return (new_momentum, update_shards, owned_update)


def solution(mesh, grid=GRID):
    placed = (P(None, "fsdp", "tensor"), P(None, "fsdp", "tensor"), P(), P(), P(), P())
    return jax.shard_map(
        functools.partial(on_device, mesh.shape["fsdp"], grid),
        mesh=mesh,
        in_specs=placed,
        out_specs=(P(None, "fsdp", "tensor"), P(None, "fsdp", "tensor"), P("fsdp", None, "tensor")),
        check_vma=False,
    )
```

time: 451 us -> 118 us (0.26); the launches traced: 446 us -> 117 us
  waiting for transfers between devices: 365 us -> 0 us
  Pallas kernels: 0 us -> 111 us
  starting transfers between devices: 32.2 us -> 0 us
  between operations: 17.5 us -> 0.66 us
  matrix products: 16.7 us -> 0 us
    unnamed x3 -> x0, waiting for transfers between devices: 220 us -> none
    pallas_call x0 -> x2, Pallas kernels: none -> 111 us  [the longest x1 108 us: on_device(): pl.pallas_call(functools.partial(step_kernel, ranks, grid), out_shape=(ja...]
    all_gather x1 -> x0, waiting for transfers between devices: 97.3 us -> none  [on_device(): gram = lax.all_gather(shares, 'tensor', axis=0, tiled=True)]
    all_to_all x2 -> x0, waiting for transfers between devices: 47.8 us -> none  [the longest x1 25.9 us: on_device(): lax.all_to_all(sent_back, 'fsdp', split_axis=0, concat_axis=0, tiled=True)]
    all_to_all x2 -> x0, starting transfers between devices: 32.1 us -> none  [the longest x1 19.4 us: on_device(): lax.all_to_all(jnp.take(blended, owned_by, axis=0), 'fsdp', split_axis=0,...]
    dot_general x9 -> x0, matrix products: 16.7 us -> none  [the longest x7 12.3 us: matmul(): jnp.dot(left_side, right_side, precision=precision, preferred_element_typ...]
  transfers between devices with their start and end apart: 4 -> 0, of which waited for: 4 -> 0; matrix products, arithmetic and copies ran while one was open for 1% -> 0% of each run, Pallas kernels for 0% -> 0%
where the time goes in v2:
time: 118 us; the launch traced here: 117 us
  Pallas kernels  111 us (94%)
  other arithmetic  3.19 us (3%)
  local copies, waits for them, and re-layouts  3.07 us (3%)
    pallas_call x1, Pallas kernels, on_device(): pl.pallas_call(functools.partial(step_kernel, ranks, grid), out_shape=(ja...  108 us
    unnamed x5, local copies, waits for them, and re-layouts  2.49 us

profile of v2, /device:TPU:1, one launch (start us, length us, event | category | flops | bytes accessed | tf_op | source)
XLA Modules:
  0.0 117.4 jit_solution(413325054492176155)
XLA Ops:
  0.6 0.0 copy-start
  0.6 0.0 copy-start.1
  0.7 0.6 copy-done.1
  1.3 0.6 dynamic-slice
  1.9 0.0 copy-done
  1.9 0.8 fusion
  2.7 0.1 iota_compare_fusion
  2.8 2.3 %add_select_fusion = f32[16,72,112]{2,1,0:T(8,128)} fusion(f32[16,72,112]{2,1,0:T(8,128)} %gradient.1, f32[16,72,112]{2,1,0:T(8,128)} %momentum.1, pred[16,72]{1,0:T(8,128)(4,1)S(1)} %iota_compare_fusion), kind=kLoop, calls=%fused_computation | loop fusion | flops 387072 | bytes 1549440 | tf_op jit(solution)/shard_map/jit(_where)/select_n | solution.py:562
  5.1 108.3 %muon_exchange.1 = (f32[16,64,128]{2,1,0:T(8,128)}, f32[576,128]{1,0:T(8,128)}) custom-call(f32[16,72,112]{2,1,0:T(8,128)} %momentum.1, f32[16,72,112]{2,1,0:T(8,128)} %gradient.1, s32[16]{0:T(128)} %live.1, s32[16]{0:T(128)} %owners.3, s32[16,16]{1,0:T(8,128)} %counts.1, s32[16,16]{1,0:T(8,128)} %offsets.1), custom_call_target="tpu_custom_call" | custom-call | tf_op jit(solution)/shard_map/muon_exchange/pallas_call | solution.py:511
  113.4 2.2 %muon_finish.1 = (f32[16,72,112]{2,1,0:T(8,128)}, f32[1,576,112]{2,1,0:T(8,128)}) custom-call(f32[16,64,128]{2,1,0:T(8,128)} %get-tuple-element.7.home, f32[576,128]{1,0:T(8,128)} %get-tuple-element.8.result, s32[16]{0:T(128)} %owners.3), custom_call_target="tpu_custom_call" | custom-call | tf_op jit(solution)/shard_map/muon_finish/pallas_call | solution.py:548
  115.6 1.8 %copy.10 = f32[1,576,112]{1,2,0:T(8,128)} copy(f32[1,576,112]{2,1,0:T(8,128)} %get-tuple-element.16) | data formatting | bytes 516096
Async XLA Ops:
  0.6 1.3 %copy-start = (s32[16,16]{1,0:T(8,128)S(1)}, s32[16,16]{1,0:T(8,128)}, u32[]{:S(2)}) copy-start(s32[16,16]{1,0:T(8,128)} %counts.1) | copy-start | bytes 3076
  0.6 0.7 copy-start.1

commit v3 on v2

--- a/solution.py
+++ b/solution.py
@@ -20,6 +20,8 @@
 QUINTIC_THIRD = 2.0315
 EPSILON = 1e-07
 SCALE = 0.2 * math.sqrt(max(INNER, WIDTH))
+
+VMEM_LIMIT = 32 * 1024 * 1024
 
 MESH = pl.DeviceIdType.MESH
 F32 = jnp.float32
@@ -156,14 +158,15 @@
 def step_kernel(
     ranks,
     grid,
-    momentum,
-    gradient,
-    live,
-    owners,
-    counts,
-    offsets,
+    momentum_out,
+    gradient_out,
+    live_out,
+    owners_out,
+    counts_out,
+    offsets_out,
     home,
     result,
+    fresh,
     sent_in,
     came_in,
     sent_out,
@@ -190,6 +193,13 @@
     x_recv,
     y_send,
     y_recv,
+    momentum,
+    gradient,
+    live,
+    owners,
+    counts,
+    offsets,
+    loads,
 ):
     y_count, x_count, core_count = grid
     matrices, slots, columns = momentum.shape
@@ -213,6 +223,23 @@
     peers = [rank_at(d) for d in range(1, ranks)] + [sibling] + x_peers + y_peers
     for peer in peers:
         pl.semaphore_signal(barrier, inc=1, device_id=peer, device_id_type=MESH)
+
+    inputs = (
+        (live_out, live),
+        (owners_out, owners),
+        (counts_out, counts),
+        (offsets_out, offsets),
+        (momentum_out, momentum),
+        (gradient_out, gradient),
+    )
+    loading = [
+        pltpu.make_async_copy(source, target, loads.at[n])
+        for n, (source, target) in enumerate(inputs)
+    ]
+    for load in loading:
+        load.start()
+    for load in loading:
+        load.wait()
 
     def owned_by(rank):
         found = jnp.int32(0)
@@ -232,10 +259,8 @@
 
     pl.semaphore_wait(barrier, len(peers))
 
-    order = near_first(ranks)
-    copies_in = {}
-    for d in order[:0:-1]:
-        copies_in[d] = pltpu.make_async_remote_copy(
+    def copy_in(d):
+        return pltpu.make_async_remote_copy(
             src_ref=sent_in.at[d],
             dst_ref=came_in.at[d],
             send_sem=in_send.at[d],
@@ -243,18 +268,31 @@
             device_id=rank_at(d),
             device_id_type=MESH,
         )
+
+    order = near_first(ranks)
+    copies_in = {d: copy_in(d) for d in range(1, ranks)}
+    for d in order[:0:-1]:
         copies_in[d].start()
+
+    rows = iota((slots, columns), 0)
+    for k in range(matrices):
+        updated = MOMENTUM_RATE * momentum[k] + gradient[k]
+        fresh[k] = jnp.where(rows < counts[k, me] * live[me], updated, 0.0)
 
     def held(rank):
         return offsets[mine, rank], counts[mine, rank] * live[rank]
 
     for pair in range(ranks // 2):
         blocks, tables = [], []
-        for d in order[2 * pair : 2 * pair + 2]:
-            if d > 0:
-                copies_in[d].wait_recv()
+        for rank in (2 * pair, 2 * pair + 1):
+            d = lax.rem(me + ranks - rank, ranks)
+
+            @pl.when(d > 0)
+            def _():
+                copy_in(d).wait_recv()
+
             blocks.append(unpack_slots(came_in[d], columns))
-            tables.append(held(lax.rem(me + ranks - d, ranks)))
+            tables.append(held(rank))
         data = jnp.concatenate(split(jnp.concatenate(blocks, axis=0)), axis=1)
         lane = iota((INNER, 2 * slots), 1)
         first = lane < slots
@@ -488,12 +526,44 @@
         copy.wait_send()
 
 
-def finish_kernel(ranks, columns, home, result, owners, update, owned):
+def finish_kernel(
+    ranks,
+    columns,
+    home,
+    result,
+    fresh,
+    owners_out,
+    new_momentum,
+    update,
+    owned,
+    update_here,
+    owned_here,
+    owners,
+    sems,
+):
     me = lax.axis_index("fsdp")
+    load = pltpu.make_async_copy(owners_out, owners, sems.at[4])
+    load.start()
+    copies = [pltpu.make_async_copy(fresh, new_momentum, sems.at[0])]
+    copies[0].start()
+    owned_here[0] = result[...].T[:columns]
+    copies.append(pltpu.make_async_copy(owned_here, owned, sems.at[1]))
+    copies[1].start()
+    load.wait()
+    half = update.shape[0] // 2
     for k in range(update.shape[0]):
         source = lax.rem(me + ranks - owners[k], ranks)
-        update[k] = unpack_slots(home[source], columns)[:, :columns]
-    owned[0] = result[:, :columns]
+        update_here[k] = unpack_slots(home[source], columns)[:, :columns]
+        if k + 1 in (half, 2 * half):
+            part = pl.ds(k + 1 - half, half)
+            copies.append(
+                pltpu.make_async_copy(
+                    update_here.at[part], update.at[part], sems.at[2 + k // half]
+                )
+            )
+            copies[-1].start()
+    for copy in copies:
+        copy.wait()
 
 
 def on_device(ranks, grid, momentum, gradient, live_ranks, owner_group, row_counts, row_offsets):
@@ -505,14 +575,19 @@
     half_rows = total_rows // core_count
 
     vmem = pl.BlockSpec(memory_space=pltpu.VMEM)
-    smem = pl.BlockSpec(memory_space=pltpu.SMEM)
+    hbm = pl.BlockSpec(memory_space=pltpu.HBM)
     packed = (ranks, slots - 8, LANES)
     dma = pltpu.SemaphoreType.DMA
-    home, result = pl.pallas_call(
+    operands = (momentum, gradient, live_ranks, owner_group, row_counts, row_offsets)
+    home, result, fresh = pl.pallas_call(
         functools.partial(step_kernel, ranks, grid),
-        out_shape=(jax.ShapeDtypeStruct(packed, F32), jax.ShapeDtypeStruct((INNER, LANES), F32)),
-        in_specs=[vmem, vmem, smem, smem, smem, smem],
-        out_specs=(vmem, vmem),
+        out_shape=(
+            jax.ShapeDtypeStruct(packed, F32),
+            jax.ShapeDtypeStruct((INNER, LANES), F32),
+            jax.ShapeDtypeStruct(momentum.shape, F32),
+        ),
+        in_specs=[hbm] * 6,
+        out_specs=(vmem, vmem, vmem),
         scratch_shapes=[
             pltpu.VMEM(packed, F32),
             pltpu.VMEM(packed, F32),
@@ -540,27 +615,41 @@
             dma((2 * y_count * x_count,)),
             dma((2 * y_count,)),
             dma((2 * y_count,)),
+            pltpu.VMEM(momentum.shape, F32),
+            pltpu.VMEM(gradient.shape, F32),
+            pltpu.SMEM(live_ranks.shape, jnp.int32),
+            pltpu.SMEM(owner_group.shape, jnp.int32),
+            pltpu.SMEM(row_counts.shape, jnp.int32),
+            pltpu.SMEM(row_offsets.shape, jnp.int32),
+            dma((6,)),
         ],
-        compiler_params=pltpu.CompilerParams(collective_id=0, has_side_effects=True),
+        compiler_params=pltpu.CompilerParams(
+            collective_id=0, has_side_effects=True, vmem_limit_bytes=VMEM_LIMIT
+        ),
         name="muon_exchange",
-    )(momentum, gradient, live_ranks, owner_group, row_counts, row_offsets)
-
-    update_shards, owned_update = pl.pallas_call(
+    )(*[pltpu.with_memory_space_constraint(each, pltpu.HBM) for each in operands])
+
+    anywhere = pl.BlockSpec(memory_space=pl.ANY)
+    flat = (1, columns, INNER)
+    new_momentum, update_shards, owned = pl.pallas_call(
         functools.partial(finish_kernel, ranks, columns),
         out_shape=(
             jax.ShapeDtypeStruct(momentum.shape, F32),
-            jax.ShapeDtypeStruct((1, INNER, columns), F32),
+            jax.ShapeDtypeStruct(momentum.shape, F32),
+            jax.ShapeDtypeStruct(flat, F32),
         ),
-        in_specs=[vmem, vmem, smem],
-        out_specs=(vmem, vmem),
+        in_specs=[vmem, vmem, vmem, hbm],
+        out_specs=(anywhere, anywhere, anywhere),
+        scratch_shapes=[
+            pltpu.VMEM(momentum.shape, F32),
+            pltpu.VMEM(flat, F32),
+            pltpu.SMEM(owner_group.shape, jnp.int32),
+            dma((5,)),
+        ],
+        compiler_params=pltpu.CompilerParams(vmem_limit_bytes=VMEM_LIMIT),
         name="muon_finish",
-    )(home, result, owner_group)
-
-    my_rank = lax.axis_index("fsdp")
-    my_counts = lax.dynamic_index_in_dim(row_counts * live_ranks[None, :], my_rank, 1, keepdims=False)
-    valid = jnp.arange(slots, dtype=jnp.int32)[None, :] < my_counts[:, None]
-    new_momentum = jnp.where(valid[:, :, None], MOMENTUM_RATE * momentum + gradient, 0.0)
-    return (new_momentum, update_shards, owned_update)
+    )(home, result, fresh, pltpu.with_memory_space_constraint(owner_group, pltpu.HBM))
+    return (new_momentum, update_shards, jnp.swapaxes(owned, 1, 2))
 
 
 def solution(mesh, grid=GRID):

time: 118 us -> 109 us (0.924)
  other arithmetic: 3.19 us -> 0 us
  local copies, waits for them, and re-layouts: 3.07 us -> 0 us
  Pallas kernels: 111 us -> 108 us
    unnamed x5 -> x0, local copies, waits for them, and re-layouts: 2.49 us -> none
    select_n x1 -> x0, other arithmetic: 2.28 us -> none  [on_device(): jnp.where(valid[:, :, None], MOMENTUM_RATE * momentum + gradient, 0.0)]
    pallas_call x1, Pallas kernels: 108 us -> 106 us  [on_device(): pl.pallas_call(functools.partial(step_kernel, ranks, grid), out_shape=(ja...]
where the time goes in v3:
time: 109 us
  Pallas kernels  108 us (99%)
    pallas_call x1, Pallas kernels, on_device(): pl.pallas_call(functools.partial(step_kernel, ranks, grid), out_shape=(ja...  106 us

profile of v3, /device:TPU:1, one launch (start us, length us, event | category | flops | bytes accessed | tf_op | source)
XLA Modules:
  0.0 108.6 jit_solution(12736362151830601361)
XLA Ops:
  0.6 106.3 %muon_exchange.1 = (f32[16,64,128]{2,1,0:T(8,128)S(1)}, f32[576,128]{1,0:T(8,128)S(1)}, f32[16,72,112]{2,1,0:T(8,128)S(1)}) custom-call(f32[16,72,112]{2,1,0:T(8,128)} %momentum_out.1, f32[16,72,112]{2,1,0:T(8,128)} %gradient_out.1, s32[16]{0:T(128)} %live_out.1, s32[16]{0:T(128)} %owners_out.3, s32[16,16]{1,0:T(8,128)} %counts_out.1, s32[16,16]{1,0:T(8,128)} %offsets_out.1), custom_call_target="tpu_custom_call" | custom-call | tf_op jit(solution)/shard_map/muon_exchange/pallas_call | solution.py:582
  107.0 1.7 %muon_finish.1 = (f32[16,72,112]{2,1,0:T(8,128)}, f32[16,72,112]{2,1,0:T(8,128)}, f32[1,112,576]{2,1,0:T(8,128)}) custom-call(f32[16,64,128]{2,1,0:T(8,128)S(1)} %get-tuple-element.9.home, f32[576,128]{1,0:T(8,128)S(1)} %get-tuple-element.10.result, f32[16,72,112]{2,1,0:T(8,128)S(1)} %get-tuple-element.11.fresh, s32[16]{0:T(128)} %owners_out.3), custom_call_target="tpu_custom_call" | custom-call | tf_op jit(solution)/shard_map/muon_finish/pallas_call | solution.py:634

commit v4 on v3

--- a/solution.py
+++ b/solution.py
@@ -21,6 +21,9 @@
 EPSILON = 1e-07
 SCALE = 0.2 * math.sqrt(max(INNER, WIDTH))
 
+STAGES = 4
+GROUPS = (0, 2, 1, 3)
+BACK_ORDER = tuple(range(16))
 VMEM_LIMIT = 32 * 1024 * 1024
 
 MESH = pl.DeviceIdType.MESH
@@ -271,8 +274,21 @@
 
     order = near_first(ranks)
     copies_in = {d: copy_in(d) for d in range(1, ranks)}
-    for d in order[:0:-1]:
-        copies_in[d].start()
+    stride = STAGES
+    strands = ranks // stride
+    far = sorted(range(strands), key=lambda i: -min(i * stride + 1, ranks - i * stride - 1))
+    for group in GROUPS:
+        nearest = lax.rem(group + ranks - me, stride)
+        for i in far:
+            d = nearest + stride * i
+            if i == 0:
+
+                @pl.when(d > 0)
+                def _():
+                    copy_in(d).start()
+
+            else:
+                copy_in(d).start()
 
     rows = iota((slots, columns), 0)
     for k in range(matrices):
@@ -425,21 +441,13 @@
                 x_send.at[slot],
                 x_recv.at[slot],
             )
-        slot = y_count + d * x_count
-        core_copies.append(
-            send(
-                home_of(back, 0), home_of(back, 0), sibling, core_send.at[slot], core_recv.at[slot]
-            )
-        )
     for d in y_order:
         back = lax.rem(y_count - d, y_count)
         for e in x_order:
             x_copies[d, e].wait_recv()
-            source = home_of(back, x_count - e)
-            slot = y_count + d * x_count + e
-            core_copies.append(
-                send(source, source, sibling, core_send.at[slot], core_recv.at[slot])
-            )
+        line = place(whole, core * cells + y_at(back) * x_count, x_count)
+        slot = y_count + d
+        core_copies.append(send(line, line, sibling, core_send.at[slot], core_recv.at[slot]))
     for copy in core_copies:
         copy.wait_recv()
 
@@ -491,11 +499,19 @@
     result[...] = final
     stack(final)
     sent = column[:PADDED, :]
-    backward = order[::-1]
-    copies_out = []
+    def copy_out(rank, d):
+        return pltpu.make_async_remote_copy(
+            src_ref=sent_out.at[rank],
+            dst_ref=home.at[d],
+            send_sem=out_send.at[d],
+            recv_sem=out_recv.at[d],
+            device_id={"fsdp": rank, "tensor": here},
+            device_id_type=MESH,
+        )
+
     for pair in range(ranks // 2):
-        ds = backward[2 * pair : 2 * pair + 2]
-        tables = [held(lax.rem(me + d, ranks)) for d in ds]
+        targets = BACK_ORDER[2 * pair : 2 * pair + 2] if ranks == 16 else (2 * pair, 2 * pair + 1)
+        tables = [held(rank) for rank in targets]
         row = iota((2 * slots, PADDED), 0)
         first = row < slots
         slot = jnp.where(first, row, row - slots)
@@ -504,22 +520,19 @@
         select = (iota((2 * slots, PADDED), 1) - slot == offset) & (slot < count)
         picked = dot(jnp.where(select, 1.0, 0.0).astype(BF16), sent)
         picked = (picked[:, :LANES] + picked[:, LANES:])[:, :columns]
-        for place, d in enumerate(ds):
-            packed = pack_slots(picked[place * slots : place * slots + slots])
-            if d == 0:
-                home[0] = packed
-                continue
-            sent_out[d] = packed
-            copy = pltpu.make_async_remote_copy(
-                src_ref=sent_out.at[d],
-                dst_ref=home.at[d],
-                send_sem=out_send.at[d],
-                recv_sem=out_recv.at[d],
-                device_id=rank_at(d),
-                device_id_type=MESH,
-            )
-            copy.start()
-            copies_out.append(copy)
+        for place, rank in enumerate(targets):
+            d = lax.rem(rank + ranks - me, ranks)
+            sent_out[rank] = pack_slots(picked[place * slots : place * slots + slots])
+
+            @pl.when(d == 0)
+            def _():
+                home[0] = sent_out[rank]
+
+            @pl.when(d > 0)
+            def _():
+                copy_out(rank, d).start()
+
+    copies_out = [copy_out(lax.rem(me + d, ranks), d) for d in range(1, ranks)]
     for copy in copies_out:
         copy.wait_recv()
     for copy in list(copies_in.values()) + pending + copies_out:

time: 109 us -> 100 us (0.917)
  the two profiles are of different devices: /device:TPU:1 before, /device:TPU:257 now
where the time goes in v4:
time: 100 us
  Pallas kernels  99.7 us (100%)
    pallas_call x1, Pallas kernels, on_device(): pl.pallas_call(functools.partial(step_kernel, ranks, grid), out_shape=(ja...  98 us

profile of v4, /device:TPU:257, one launch (start us, length us, event | category | flops | bytes accessed | tf_op | source)
XLA Modules:
  0.0 100.3 jit_solution(9517356480054654720)
XLA Ops:
  0.6 98.0 %muon_exchange.1 = (f32[16,64,128]{2,1,0:T(8,128)S(1)}, f32[576,128]{1,0:T(8,128)S(1)}, f32[16,72,112]{2,1,0:T(8,128)S(1)}) custom-call(f32[16,72,112]{2,1,0:T(8,128)} %momentum_out.1, f32[16,72,112]{2,1,0:T(8,128)} %gradient_out.1, s32[16]{0:T(128)} %live_out.1, s32[16]{0:T(128)} %owners_out.3, s32[16,16]{1,0:T(8,128)} %counts_out.1, s32[16,16]{1,0:T(8,128)} %offsets_out.1), custom_call_target="tpu_custom_call" | custom-call | tf_op jit(solution)/shard_map/muon_exchange/pallas_call | solution.py:595
  98.6 1.7 %muon_finish.1 = (f32[16,72,112]{2,1,0:T(8,128)}, f32[16,72,112]{2,1,0:T(8,128)}, f32[1,112,576]{2,1,0:T(8,128)}) custom-call(f32[16,64,128]{2,1,0:T(8,128)S(1)} %get-tuple-element.9.home, f32[576,128]{1,0:T(8,128)S(1)} %get-tuple-element.10.result, f32[16,72,112]{2,1,0:T(8,128)S(1)} %get-tuple-element.11.fresh, s32[16]{0:T(128)} %owners_out.3), custom_call_target="tpu_custom_call" | custom-call | tf_op jit(solution)/shard_map/muon_finish/pallas_call | solution.py:647

commit v5 on v4

--- a/solution.py
+++ b/solution.py
@@ -474,26 +474,32 @@
 
     start = (gathered[:, :LANES] + gathered[:, LANES:]) * inverse
     kept[...] = start
-    summed[...] = jnp.zeros_like(start)
     stack(start)
 
-    @pl.loop(0, 12)
-    def _(index):
-        phase = lax.rem(index + 3, 5)
-        opens = (phase == 3) | (phase == 1)
-        closes = (phase == 4) | (phase == 2)
-        keep_part = jnp.where(opens, QUINTIC_SECOND, jnp.where(closes, QUINTIC_FIRST, 0.0))
-        product_part = jnp.where(opens, QUINTIC_THIRD, 1.0)
-        sum_part = jnp.where(
-            index == 1,
-            QUINTIC_FIRST,
-            jnp.where(index == 6, QUINTIC_SECOND, jnp.where(index == 11, QUINTIC_THIRD, 0.0)),
-        )
-        product = dot(halves[...], column[...])
-        value = keep_part * kept[...] + product_part * (product[:, :LANES] + product[:, LANES:])
+    def product():
+        both = dot(halves[...], column[...])
+        return both[:, :LANES] + both[:, LANES:]
+
+    def polynomial():
+        stack(QUINTIC_SECOND * kept[...] + QUINTIC_THIRD * product())
+        return QUINTIC_FIRST * kept[...] + product()
+
+    value = polynomial()
+    kept[...] = value
+    summed[...] = QUINTIC_FIRST * value
+    stack(value)
+
+    @pl.loop(0, 2)
+    def _(turn):
+        value = product()
+        kept[...] = value
         stack(value)
-        kept[...] = jnp.where(opens, kept[...], value)
-        summed[...] += sum_part * value
+        value = polynomial()
+        kept[...] = value
+        stack(value)
+        value = polynomial()
+        stack(value)
+        summed[...] += jnp.where(turn == 0, QUINTIC_SECOND, QUINTIC_THIRD) * value
 
     final = summed[...] * SCALE
     result[...] = final

time: 100 us -> 103 us (1.030)
  Pallas kernels: 99.7 us -> 102 us
    pallas_call x1, Pallas kernels: 98 us -> 100 us  [on_device(): pl.pallas_call(functools.partial(step_kernel, ranks, grid), out_shape=(ja...]
where the time goes in v5:
time: 103 us; the launch traced here: 102 us
  Pallas kernels  102 us (99%)
    pallas_call x1, Pallas kernels, on_device(): pl.pallas_call(functools.partial(step_kernel, ranks, grid), out_shape=(ja...  100 us

profile of v5, /device:TPU:257, one launch (start us, length us, event | category | flops | bytes accessed | tf_op | source)
XLA Modules:
  0.0 102.4 jit_solution(15793460941232119432)
XLA Ops:
  0.6 100.1 %muon_exchange.1 = (f32[16,64,128]{2,1,0:T(8,128)S(1)}, f32[576,128]{1,0:T(8,128)S(1)}, f32[16,72,112]{2,1,0:T(8,128)S(1)}) custom-call(f32[16,72,112]{2,1,0:T(8,128)} %momentum_out.1, f32[16,72,112]{2,1,0:T(8,128)} %gradient_out.1, s32[16]{0:T(128)} %live_out.1, s32[16]{0:T(128)} %owners_out.3, s32[16,16]{1,0:T(8,128)} %counts_out.1, s32[16,16]{1,0:T(8,128)} %offsets_out.1), custom_call_target="tpu_custom_call" | custom-call | tf_op jit(solution)/shard_map/muon_exchange/pallas_call | solution.py:601
  100.8 1.7 %muon_finish.1 = (f32[16,72,112]{2,1,0:T(8,128)}, f32[16,72,112]{2,1,0:T(8,128)}, f32[1,112,576]{2,1,0:T(8,128)}) custom-call(f32[16,64,128]{2,1,0:T(8,128)S(1)} %get-tuple-element.9.home, f32[576,128]{1,0:T(8,128)S(1)} %get-tuple-element.10.result, f32[16,72,112]{2,1,0:T(8,128)S(1)} %get-tuple-element.11.fresh, s32[16]{0:T(128)} %owners_out.3), custom_call_target="tpu_custom_call" | custom-call | tf_op jit(solution)/shard_map/muon_finish/pallas_call | solution.py:653
